TPU v7x, 32 devices: a whole 2x2x4 slice. The times are simulated.
32 devices in a mesh: dp: 4 (over y, x), mp: 8 (over z, core).
Axes of the slice: x: 2, y: 2, z: 4, core: 2. Of those that a mesh axis runs over, the one named last changes fastest.
Arguments:
- tokens: bfloat16 [8192, 2048], P(('dp', 'mp')), may hold values from -6 to 6
- ln1_gain: float32 [2048], replicated, may hold values from 0.5 to 1.5
- ln1_bias: float32 [2048], replicated, may hold values from -1.75 to 1.75
- w_query: bfloat16 [2048, 2048], P(None, 'mp'), may hold values from -0.125 to 0.125
- b_query: float32 [2048], P('mp'), may hold values from -3 to 3
- w_key: bfloat16 [2048, 2048], P(None, 'mp'), may hold values from -0.125 to 0.125
- w_value: bfloat16 [2048, 2048], P(None, 'mp'), may hold values from -0.125 to 0.125
- b_value: float32 [2048], P('mp'), may hold values from -0.125 to 0.125
- w_out: bfloat16 [2048, 2048], P('mp'), may hold values from -2 to 2
- b_out: float32 [2048], replicated, may hold values from -3 to 3
- ln2_gain: float32 [2048], replicated, may hold values from 0.5 to 1.5
- ln2_bias: float32 [2048], replicated, may hold values from -1.75 to 1.75
- w_up: bfloat16 [2048, 8192], P(None, 'mp'), may hold values from -0.125 to 0.125
- b_up: float32 [8192], P('mp'), may hold values from -3 to 3
- w_down: bfloat16 [8192, 2048], P('mp'), may hold values from -0.0625 to 0.0625
- b_down: float32 [2048], replicated, may hold values from -3 to 3
- cotangent: bfloat16 [8192, 2048], P(('dp', 'mp')), may hold values from -6 to 6
- seq_ids: int32 [4, 2048], P('dp'), may hold values from 0 to 2, as said below
- block_mask: int32 [4, 8, 8], P('dp'), may hold values from 0 to 1, as said below
- counts: int32 [4], replicated, may hold values from 512 to 2048, as said below
Outputs:
- output: float32 [8192, 2048], P(('dp', 'mp'))
- grad_in: float32 [8192, 2048], P(('dp', 'mp'))
- grad_ln1_gain: float32 [2048], replicated
- grad_ln1_bias: float32 [2048], replicated
- grad_w_query: float32 [2048, 2048], P(None, 'mp')
- grad_b_query: float32 [2048], P('mp')
- grad_w_key: float32 [2048, 2048], P(None, 'mp')
- grad_w_value: float32 [2048, 2048], P(None, 'mp')
- grad_b_value: float32 [2048], P('mp')
- grad_w_out: float32 [2048, 2048], P('mp')
- grad_b_out: float32 [2048], replicated
- grad_ln2_gain: float32 [2048], replicated
- grad_ln2_bias: float32 [2048], replicated
- grad_w_up: float32 [2048, 8192], P(None, 'mp')
- grad_b_up: float32 [8192], P('mp')
- grad_w_down: float32 [8192, 2048], P('mp')
- grad_b_down: float32 [2048], replicated
Inputs may be any that keep to these rules, and one draw needn't show every extreme that they name: `counts`: one group's count equals 2048 in every draw. `seq_ids`: in group g, slots before a cut carry 0, slots from the cut up to counts[g] - 1 carry 1, later slots carry 2; the cut lies between max(counts[g] - 2048, counts[g] // 2) and min(counts[g], 2048). `block_mask`: diagonal entries are 1 and entries above the diagonal are 0.
All inputs are finite; a program needn't handle non-finite values.
Results may differ from a plain program's by a relative error of at most 0.012.
Values may be sent and summed in bfloat16 or wider, within the bound.
No kernel may reach another device: no remote copies, remote signals or barrier semaphores. Data moves between devices by JAX's collectives and lax.ppermute only.
A program may use at most 256 MiB of HBM per device.

v0:
```python
import jax
import jax.numpy as jnp
from jax import lax
from jax.sharding import PartitionSpec as P

HD = 128
BLOCK = 256
epsilon = 1e-05


def layer_norm(values, gain, bias):
    average = jnp.mean(values, axis=-1, keepdims=True)
    centered = values - average
    variance = jnp.mean(centered * centered, axis=-1, keepdims=True)
    return centered * lax.rsqrt(variance + epsilon) * gain + bias


def inner_rows(left, right):
    return lax.dot_general(
        left, right, (((0,), (0,)), ((), ())), preferred_element_type=jnp.float32
    )


def times_transpose(left, right):
    return lax.dot_general(
        left, right, (((1,), (1,)), ((), ())), preferred_element_type=jnp.float32
    )


def allowed_rows(offset, number, seq_row, mask_table):
    group_tokens = seq_row.shape[0]
    table_width = mask_table.shape[1]
    query_pos = offset + jnp.arange(number, dtype=jnp.int32)
    key_pos = jnp.arange(group_tokens, dtype=jnp.int32)
    query_seq = lax.dynamic_slice_in_dim(seq_row, offset, number)
    table_rows = lax.dynamic_slice_in_dim(mask_table, offset // BLOCK, number // BLOCK, 0)
    spread = jnp.broadcast_to(
        table_rows[:, None, :, None], (number // BLOCK, BLOCK, table_width, BLOCK)
    ).reshape(number, group_tokens)
    return (
        (key_pos[None, :] <= query_pos[:, None])
        & (query_seq[:, None] == seq_row[None, :])
        & (spread == 1)
    )


def on_device(
    tokens,
    ln1_gain,
    ln1_bias,
    w_query,
    b_query,
    w_key,
    w_value,
    b_value,
    w_out,
    b_out,
    ln2_gain,
    ln2_bias,
    w_up,
    b_up,
    w_down,
    b_down,
    cotangent,
    seq_ids,
    block_mask,
    counts,
):
    row_count = tokens.shape[0]
    mp_size = lax.axis_size("mp")
    group_tokens = row_count * mp_size
    local_width = w_query.shape[1]
    local_heads = local_width // HD
    span = min(512, group_tokens)
    block_total = group_tokens // span
    scaling = HD ** (-0.5)
    seq_row = seq_ids[0]
    mask_table = block_mask[0]
    head_shape = (group_tokens, local_heads, HD)
    inputs = tokens.astype(jnp.float32)
    normed_float, pull_one = jax.vjp(layer_norm, inputs, ln1_gain, ln1_bias)
    normed_one = normed_float.astype(jnp.bfloat16)
    gathered_one = lax.all_gather(normed_one, "mp", axis=0, tiled=True)
    queries = (
        (jnp.dot(gathered_one, w_query, preferred_element_type=jnp.float32) + b_query)
        .astype(jnp.bfloat16)
        .reshape(head_shape)
    )
    key_rows = (
        jnp.dot(gathered_one, w_key, preferred_element_type=jnp.float32)
        .astype(jnp.bfloat16)
        .reshape(head_shape)
    )
    values = (
        (jnp.dot(gathered_one, w_value, preferred_element_type=jnp.float32) + b_value)
        .astype(jnp.bfloat16)
        .reshape(head_shape)
    )

    def forward_block(block_index):
        offset = block_index * span
        query_block = lax.dynamic_slice_in_dim(queries, offset, span, 0)
        scores = (
            jnp.einsum("qhd,khd->hqk", query_block, key_rows, preferred_element_type=jnp.float32)
            * scaling
        )
        allowed = allowed_rows(offset, span, seq_row, mask_table)
        scores = jnp.where(allowed[None], scores, -1e30)
        largest = jnp.max(scores, axis=-1, keepdims=True)
        exponent = jnp.exp(scores - largest)
        totals = jnp.sum(exponent, axis=-1, keepdims=True)
        weights = exponent / totals
        mixed = jnp.einsum(
            "hqk,khd->qhd", weights.astype(jnp.bfloat16), values, preferred_element_type=jnp.float32
        )
        return (
            mixed.reshape(span, local_width).astype(jnp.bfloat16),
            (largest + jnp.log(totals))[..., 0],
        )

    attended_blocks, log_totals = lax.map(forward_block, jnp.arange(block_total, dtype=jnp.int32))
    attended = attended_blocks.reshape(group_tokens, local_width)
    branch = lax.psum_scatter(
        jnp.dot(attended, w_out, preferred_element_type=jnp.float32),
        "mp",
        scatter_dimension=0,
        tiled=True,
    )
    middle = inputs + branch + b_out
    normed_mid, pull_two = jax.vjp(layer_norm, middle, ln2_gain, ln2_bias)
    normed_two = normed_mid.astype(jnp.bfloat16)
    gathered_two = lax.all_gather(normed_two, "mp", axis=0, tiled=True)
    hidden = jnp.dot(gathered_two, w_up, preferred_element_type=jnp.float32) + b_up
    activated_float, pull_gelu = jax.vjp(lambda point: jax.nn.gelu(point, approximate=True), hidden)
    activated = activated_float.astype(jnp.bfloat16)
    result = (
        middle
        + lax.psum_scatter(
            jnp.dot(activated, w_down, preferred_element_type=jnp.float32).astype(jnp.bfloat16),
            "mp",
            scatter_dimension=0,
            tiled=True,
        ).astype(jnp.float32)
        + b_down
    )
    group_index = lax.axis_index("dp")
    place = lax.axis_index("mp")
    dp_size = counts.shape[0]
    count_float = counts.astype(jnp.float32)
    is_here = jnp.arange(dp_size, dtype=jnp.int32) == group_index
    count_here = jnp.sum(jnp.where(is_here, counts, 0))
    weighting = dp_size * jnp.sum(jnp.where(is_here, count_float, 0.0)) / jnp.sum(count_float)
    positions = place * row_count + jnp.arange(row_count, dtype=jnp.int32)
    valid_rows = (positions < count_here).astype(jnp.float32)
    out_cot = cotangent.astype(jnp.float32) * valid_rows[:, None] * weighting
    grad_down_bias = jnp.sum(out_cot, axis=0)
    out_cot_low = out_cot.astype(jnp.bfloat16)
    gathered_cot = lax.all_gather(out_cot_low, "mp", axis=0, tiled=True)
    activated_cot = times_transpose(gathered_cot, w_down)
    grad_down = inner_rows(activated, gathered_cot)
    hidden_cot = pull_gelu(activated_cot)[0].astype(jnp.bfloat16)
    grad_up = inner_rows(gathered_two, hidden_cot)
    grad_up_bias = jnp.sum(hidden_cot, axis=0, dtype=jnp.float32)
    normed_two_cot = lax.psum_scatter(
        times_transpose(hidden_cot, w_up), "mp", scatter_dimension=0, tiled=True
    )
    middle_part, grad_gain_two, grad_bias_two = pull_two(normed_two_cot)
    middle_cot = out_cot + middle_part
    grad_out_bias = jnp.sum(middle_cot, axis=0)
    branch_cot = middle_cot.astype(jnp.bfloat16)
    gathered_branch = lax.all_gather(branch_cot, "mp", axis=0, tiled=True)
    attended_cot = times_transpose(gathered_branch, w_out).astype(jnp.bfloat16)
    grad_out = inner_rows(attended, gathered_branch)
    attended_cot = attended_cot.reshape(head_shape)

    def backward_block(carry, block_index):
        key_grad, value_grad = carry
        offset = block_index * span
        query_block = lax.dynamic_slice_in_dim(queries, offset, span, 0)
        cot_block = lax.dynamic_slice_in_dim(attended_cot, offset, span, 0)
        log_here = lax.dynamic_index_in_dim(log_totals, block_index, 0, keepdims=False)
        scores = (
            jnp.einsum("qhd,khd->hqk", query_block, key_rows, preferred_element_type=jnp.float32)
            * scaling
        )
        allowed = allowed_rows(offset, span, seq_row, mask_table)
        weights = jnp.where(allowed[None], jnp.exp(scores - log_here[..., None]), 0.0)
        weight_cot = jnp.einsum(
            "qhd,khd->hqk", cot_block, values, preferred_element_type=jnp.float32
        )
        centre = jnp.sum(weights * weight_cot, axis=-1, keepdims=True)
        score_cot = (weights * (weight_cot - centre)).astype(jnp.bfloat16)
        query_grad = (
            jnp.einsum("hqk,khd->qhd", score_cot, key_rows, preferred_element_type=jnp.float32)
            * scaling
        )
        key_grad = (
            key_grad
            + jnp.einsum("hqk,qhd->khd", score_cot, query_block, preferred_element_type=jnp.float32)
            * scaling
        )
        value_grad = value_grad + jnp.einsum(
            "hqk,qhd->khd",
            weights.astype(jnp.bfloat16),
            cot_block,
            preferred_element_type=jnp.float32,
        )
        return ((key_grad, value_grad), query_grad)

    zeros_start = jnp.zeros(head_shape, jnp.float32)
    (key_grad, value_grad), query_blocks = lax.scan(
        backward_block, (zeros_start, zeros_start), jnp.arange(block_total, dtype=jnp.int32)
    )
    query_low = query_blocks.reshape(group_tokens, local_width).astype(jnp.bfloat16)
    key_low = key_grad.reshape(group_tokens, local_width).astype(jnp.bfloat16)
    value_low = value_grad.reshape(group_tokens, local_width).astype(jnp.bfloat16)
    grad_query = inner_rows(gathered_one, query_low)
    grad_query_bias = jnp.sum(query_low, axis=0, dtype=jnp.float32)
    grad_key = inner_rows(gathered_one, key_low)
    grad_value = inner_rows(gathered_one, value_low)
    grad_value_bias = jnp.sum(value_low, axis=0, dtype=jnp.float32)
    normed_one_cot = lax.psum_scatter(
        times_transpose(query_low, w_query)
        + times_transpose(key_low, w_key)
        + times_transpose(value_low, w_value),
        "mp",
        scatter_dimension=0,
        tiled=True,
    )
    input_part, grad_gain_one, grad_bias_one = pull_one(normed_one_cot)
    grad_input = middle_cot + input_part
    small = lax.psum(
        (grad_gain_one, grad_bias_one, grad_out_bias, grad_gain_two, grad_bias_two, grad_down_bias),
        ("dp", "mp"),
    )
    large = lax.psum(
        (
            grad_query,
            grad_query_bias,
            grad_key,
            grad_value,
            grad_value_bias,
            grad_out,
            grad_up,
            grad_up_bias,
            grad_down,
        ),
        "dp",
    )
    return (
        result,
        grad_input,
        small[0],
        small[1],
        large[0],
        large[1],
        large[2],
        large[3],
        large[4],
        large[5],
        small[2],
        small[3],
        small[4],
        large[6],
        large[7],
        large[8],
        small[5],
    )


def solution(mesh):
    return jax.shard_map(
        on_device,
        mesh=mesh,
        in_specs=(
            P(("dp", "mp"), None),
            P(),
            P(),
            P(None, "mp"),
            P("mp"),
            P(None, "mp"),
            P(None, "mp"),
            P("mp"),
            P("mp", None),
            P(),
            P(),
            P(),
            P(None, "mp"),
            P("mp"),
            P("mp", None),
            P(),
            P(("dp", "mp"), None),
            P("dp", None),
            P("dp", None, None),
            P(),
        ),
        out_specs=(
            P(("dp", "mp"), None),
            P(("dp", "mp"), None),
            P(),
            P(),
            P(None, "mp"),
            P("mp"),
            P(None, "mp"),
            P(None, "mp"),
            P("mp"),
            P("mp", None),
            P(),
            P(),
            P(),
            P(None, "mp"),
            P("mp"),
            P("mp", None),
            P(),
        ),
        check_vma=False,
    )
```

profile of v0, /device:TPU:0, one launch (start us, length us, event | category | flops | bytes accessed | tf_op | source)
XLA Modules:
  0.0 1679.2 jit_solution(10199350876054711192)
XLA Ops:
  14.4 84.8 %all-gather.5.cloned.1.call-done = bf16[2048,2048]{1,0:T(8,128)(2,1)} async-done(((bf16[256,2048]{1,0:T(8,128)(2,1)}), bf16[2048,2048]{1,0:T(8,128)(2,1)}) %all-gather.5.cloned.1.call-update) | async-done | bytes 8388624 | tf_op jit(solution)/shard_map/all_gather | solution.py:83
  99.2 6.7 convolution_convert_fusion.2
  107.6 6.7 fusion.51
  116.0 7.0 fusion.52
  123.0 54.4 %while.31 = (s32[]{:T(128)}, bf16[4,512,256]{2,1,0:T(8,128)(2,1)}, f32[4,2,512]{2,1,0:T(2,128)S(1)}, s32[4]{0:T(128)S(1)}, s32[2048]{0:T(1024)S(1)}, /*index=5*/...) while((s32[]{:T(128)}, bf16[4,512,256]{2,1,0:T(8,128)(2,1)}, ...), condition=%wide.region_5.6_spmd, body=%wide.region_2.5_spmd.sunk | while | flops 1103232512 | bytes 41470496 | solution.py:121
  177.4 9.7 fusion.82
  187.2 166.7 %reduce-scatter.5.cloned.1.call-done = f32[256,2048]{1,0:T(8,128)} async-done(((f32[2048,2048]{1,0:T(8,128)}), f32[256,2048]{1,0:T(8,128)}) %reduce-scatter.5.cloned.1.call-update) | async-done | bytes 2097168 | tf_op jit(solution)/shard_map/reduce_scatter | solution.py:123
  363.3 76.0 %all-gather.7.cloned.1.call-done = bf16[2048,2048]{1,0:T(8,128)(2,1)} async-done(((bf16[256,2048]{1,0:T(8,128)(2,1)}), bf16[2048,2048]{1,0:T(8,128)(2,1)}) %all-gather.7.cloned.1.call-update) | async-done | bytes 8388624 | tf_op jit(solution)/shard_map/all_gather | solution.py:132
  439.3 14.7 fusion.83
  454.0 67.9 %all-gather.9.cloned.1.call-done = bf16[2048,2048]{1,0:T(8,128)(2,1)} async-done(((bf16[256,2048]{1,0:T(8,128)(2,1)}), bf16[2048,2048]{1,0:T(8,128)(2,1)}) %all-gather.9.cloned.1.call-update) | async-done | bytes 8388624 | tf_op jit(solution)/shard_map/all_gather | solution.py:158
  521.9 20.8 %convert_reduce_fusion = (f32[1024]{0:T(1024)}, bf16[2048,1024]{1,0:T(8,128)(2,1)S(1)}) fusion(f32[2048,1024]{1,0:T(8,128)} %fusion.83, f32[1024]{0:T(1024)S(1)} %copy-done.50, bf16[2048,2048]{1,0:T(8,128)(2,1)} %all-gather.9.cloned.1.call-done, bf16[1024,2048]{1,0:T(8,128)(2,1)} %param.38), kind=kOutput, calls=%fused_computation.62 | convolution fusion | flops 8638168064 | bytes 25174016 | tf_op jit(solution)/shard_map/dot_general | solution.py:25
  544.8 12.3 fusion.84
  557.1 15.4 convolution_convert_fusion
  572.6 151.2 %reduce-scatter.9.cloned.1.call-done = f32[256,2048]{1,0:T(8,128)} async-done(((f32[2048,2048]{1,0:T(8,128)}), f32[256,2048]{1,0:T(8,128)}) %reduce-scatter.9.cloned.1.call-update) | async-done | bytes 2097168 | tf_op jit(solution)/shard_map/reduce_scatter | solution.py:164
  727.4 87.2 %reduce-scatter.7.cloned.1.call-done = bf16[256,2048]{1,0:T(8,128)(2,1)} async-done(((bf16[2048,2048]{1,0:T(8,128)(2,1)}), bf16[256,2048]{1,0:T(8,128)(2,1)}) %reduce-scatter.7.cloned.1.call-update) | async-done | bytes 1048592 | tf_op jit(solution)/shard_map/reduce_scatter | solution.py:138
  814.6 4.5 fusion.79
  823.8 78.8 %all-gather.11.cloned.1.call-done = bf16[2048,2048]{1,0:T(8,128)(2,1)} async-done(((bf16[256,2048]{1,0:T(8,128)(2,1)}), bf16[2048,2048]{1,0:T(8,128)(2,1)}) %all-gather.11.cloned.1.call-update) | async-done | bytes 8388624 | tf_op jit(solution)/shard_map/all_gather | solution.py:171
  902.6 6.7 convolution_convert_fusion.1
  909.3 88.9 %while.32 = (s32[]{:T(128)}, f32[2048,2,128]{0,2,1:T(8,128)}, f32[2048,2,128]{0,2,1:T(8,128)}, bf16[4,512,2,128]{3,1,2,0:T(8,128)(2,1)}, s32[4]{0:T(128)S(1)}, /...) while((s32[]{:T(128)}, f32[2048,2,128]{0,2,1:T(8,128)}, ...), condition=%wide.region_18.19_spmd.clone, body=%wide.region_16.18_spmd.clone.sunk | while | flops 2722758144 | bytes 118012680 | solution.py:211
  937.5 4.8 fusion.169
  960.0 4.8 fusion.169
  982.5 4.8 fusion.169
  1004.2 8.2 fusion.85
  1012.4 8.1 fusion.65
  1020.6 18.4 %add_add_fusion = f32[2048,2048]{1,0:T(8,128)} fusion(f32[2048,2048]{1,0:T(8,128)} %fusion.65, f32[2048,2048]{1,0:T(8,128)} %fusion.85, bf16[2048,256]{0,1:T(8,128)(2,1)S(1)} %bitcast.145, bf16[2048,256]{1,0:T(8,128)(2,1)} %param.30), kind=kOutput, calls=%fused_computation.52 | convolution fusion | flops 2155872256 | bytes 52428800 | tf_op jit(solution)/shard_map/dot_general | solution.py:25
  1039.1 15.2 fusion.89
  1054.4 19.1 %fusion.76 = f32[1024,2048]{1,0:T(8,128)} fusion(bf16[2048,2048]{1,0:T(8,128)(2,1)} %all-gather.9.cloned.1.call-done, f32[2048,1024]{1,0:T(8,128)} %fusion.83, f32[1024]{0:T(1024)S(1)} %copy-done.51), kind=kOutput, calls=%fused_computation.125 | convolution fusion | flops 8610906112 | bytes 25169920 | tf_op jit(solution)/shard_map/dot_general | solution.py:19
  1073.6 7.2 fusion.88
  1093.8 10.9 all-reduce.1
  1104.7 101.2 %reduce-scatter.11.cloned.1.call-done = f32[256,2048]{1,0:T(8,128)} async-done(((f32[2048,2048]{1,0:T(8,128)}), f32[256,2048]{1,0:T(8,128)}) %reduce-scatter.11.cloned.1.call-update) | async-done | bytes 2097168 | tf_op jit(solution)/shard_map/reduce_scatter | solution.py:222
  1213.4 40.2 %all-reduce = (f32[2048]{0:T(1024)}, f32[2048]{0:T(1024)}, f32[2048]{0:T(1024)}, f32[2048]{0:T(1024)}, f32[2048]{0:T(1024)}, /*index=5*/f32[2048]{0:T(1024)}) all-reduce(f32[2048]{0:T(1024)S(1)} %get-tuple-element.403, f32[2048]{0:T(1024)S(1)} %get-tuple-element.406, ...), channel_id=1, replica_groups=mesh['dp'=4,'mp'=8] {'dp','mp'}, use_global_device_ids=true, to_apply=%region_23.24 | all-reduce | flops 12288 | bytes 98304 | tf_op jit(solution)/shard_map/psum | solution.py:232
  1253.6 400.9 %all-reduce.5.cloned.1.call-done = (f32[2048,256]{1,0:T(8,128)}, f32[2048,256]{1,0:T(8,128)}, f32[2048,256]{1,0:T(8,128)}, f32[256,2048]{1,0:T(8,128)}, f32[2048,1024]{1,0:T(8,128)}, /*index=5*/f32[1024,2048]{1,0:T(8,128)}) async-done(((f32[2048,256]{1,0:T(8,128)}, f32[2048,256]{1,0:T(8,128)}, f32[2048,256]{1,0:T(8,128)}, f32[256,2048]{1,0:T(8,128)}, f32[2048,1024]{1,0:T(8,128)}, ...) | async-done | bytes 25165840 | tf_op jit(solution)/shard_map/psum | solution.py:236
  (336 shorter events, 187.9 us)
Async XLA Ops:
  7.2 170.2 %copy-start = (bf16[256,2048]{1,0:T(8,128)(2,1)S(1)}, bf16[256,2048]{1,0:T(8,128)(2,1)}, u32[]{:S(2)}) copy-start(bf16[256,2048]{1,0:T(8,128)(2,1)} %param.32) | copy-start | bytes 3145732
  7.2 92.0 %copy-start.24 = (bf16[2048,256]{1,0:T(8,128)(2,1)S(1)}, bf16[2048,256]{1,0:T(8,128)(2,1)}, u32[]{:S(2)}) copy-start(bf16[2048,256]{1,0:T(8,128)(2,1)} %param.29) | copy-start | bytes 3145732
  7.2 92.0 %all-gather.5.cloned.1.call-start = ((), (), s32[]{:S(2)}) async-start(), calls=%async_computation.4 | async-start | bytes 9437184 | tf_op jit(solution)/shard_map/all_gather | solution.py:83
  14.3 339.6 %reduce-scatter.5.cloned.1.call-start = ((), (), s32[]{:S(2)}) async-start(), calls=%async_computation.5 | async-start | bytes 18874368 | tf_op jit(solution)/shard_map/reduce_scatter | solution.py:123
  14.4 93.2 %copy-start.26 = (bf16[2048,256]{1,0:T(8,128)(2,1)S(1)}, bf16[2048,256]{1,0:T(8,128)(2,1)}, u32[]{:S(2)}) copy-start(bf16[2048,256]{1,0:T(8,128)(2,1)} %param.27) | copy-start | bytes 3145732
  14.4 93.2 %copy-start.52 = (f32[256]{0:T(256)S(1)}, f32[256]{0:T(256)}, u32[]{:S(2)}) copy-start(f32[256]{0:T(256)} %param.28) | copy-start | bytes 3076
  187.1 166.8 %copy-start.5 = (bf16[256,2048]{1,0:T(8,128)(2,1)S(1)}, bf16[256,2048]{1,0:T(8,128)(2,1)}, u32[]{:S(2)}) copy-start(bf16[256,2048]{1,0:T(8,128)(2,1)} %param.24) | copy-start | bytes 3145732
  187.1 166.8 %copy-start.44 = (f32[2048]{0:T(1024)S(1)}, f32[2048]{0:T(1024)}, u32[]{:S(2)}) copy-start(f32[2048]{0:T(1024)} %param.33) | copy-start | bytes 24580
  187.1 170.1 %copy-start.30 = (f32[2048]{0:T(1024)S(1)}, f32[2048]{0:T(1024)}, u32[]{:S(2)}) copy-start(f32[2048]{0:T(1024)} %param.34) | copy-start | bytes 24580
  187.1 170.1 %copy-start.45 = (f32[2048]{0:T(1024)S(1)}, f32[2048]{0:T(1024)}, u32[]{:S(2)}) copy-start(f32[2048]{0:T(1024)} %param.35) | copy-start | bytes 24580
  187.1 252.2 %all-gather.7.cloned.1.call-start = ((), (), s32[]{:S(2)}) async-start(), calls=%async_computation.6 | async-start | bytes 9437184 | tf_op jit(solution)/shard_map/all_gather | solution.py:132
  358.6 163.2 %all-gather.9.cloned.1.call-start = ((), (), s32[]{:S(2)}) async-start(), calls=%async_computation.8 | async-start | bytes 9437184 | tf_op jit(solution)/shard_map/all_gather | solution.py:158
  362.0 457.2 %copy-start.38 = (f32[256]{0:T(256)}, f32[256]{0:T(256)S(1)}, u32[]{:S(2)}) copy-start(f32[256]{0:T(256)S(1)} %compare_convert_fusion) | copy-start | bytes 3076
  363.3 158.6 %copy-start.50 = (f32[1024]{0:T(1024)S(1)}, f32[1024]{0:T(1024)}, u32[]{:S(2)}) copy-start(f32[1024]{0:T(1024)} %param.37) | copy-start | bytes 12292
  363.3 360.6 %reduce-scatter.9.cloned.1.call-start = ((), (), s32[]{:S(2)}) async-start(), calls=%async_computation.9 | async-start | bytes 18874368 | tf_op jit(solution)/shard_map/reduce_scatter | solution.py:164
  521.9 22.9 %copy-start.49 = (bf16[2048,1024]{1,0:T(8,128)(2,1)S(1)}, bf16[2048,1024]{1,0:T(8,128)(2,1)}, u32[]{:S(2)}) copy-start(bf16[2048,1024]{1,0:T(8,128)(2,1)} %param.36) | copy-start | bytes 12582916
  557.1 257.5 %reduce-scatter.7.cloned.1.call-start = ((), (), s32[]{:S(2)}) async-start(), calls=%async_computation.7 | async-start | bytes 9437184 | tf_op jit(solution)/shard_map/reduce_scatter | solution.py:138
  572.6 242.0 %copy-start.46 = (f32[2048]{0:T(1024)S(1)}, f32[2048]{0:T(1024)}, u32[]{:S(2)}) copy-start(f32[2048]{0:T(1024)} %param.39) | copy-start | bytes 24580
  572.6 330.0 %all-gather.11.cloned.1.call-start = ((), (), s32[]{:S(2)}) async-start(), calls=%async_computation.10 | async-start | bytes 9437184 | tf_op jit(solution)/shard_map/all_gather | solution.py:171
  819.1 90.2 %copy-start.42 = (f32[256]{0:T(256)}, f32[256]{0:T(256)S(1)}, u32[]{:S(2)}) copy-start(f32[256]{0:T(256)S(1)} %negate_multiply_fusion.1) | copy-start | bytes 3076
  821.9 383.9 %reduce-scatter.11.cloned.1.call-start = ((), (), s32[]{:S(2)}) async-start(), calls=%async_computation.11 | async-start | bytes 18874368 | tf_op jit(solution)/shard_map/reduce_scatter | solution.py:222
  1039.1 615.4 %all-reduce.5.cloned.1.call-start = ((), (), s32[]{:S(2)}) async-start(), calls=%async_computation.12 | async-start | bytes 50331648 | tf_op jit(solution)/shard_map/psum | solution.py:236
  1039.1 41.6 %slice-start.4 = ((s8[8388608]{0:T(1024)(128)(4,1)}), s8[4194304]{0:T(1024)(128)(4,1)S(1)}, s32[]{:S(2)}) async-start(s8[8388608]{0:T(1024)(128)(4,1)} %bitcast.162), calls=%async_computation.17 | async-start | bytes 8388608
  1054.4 26.4 %slice-start.5 = ((s8[8388608]{0:T(1024)(128)(4,1)}), s8[4194304]{0:T(1024)(128)(4,1)S(1)}, s32[]{:S(2)}) async-start(s8[8388608]{0:T(1024)(128)(4,1)} %bitcast.162), calls=%async_computation.18 | async-start | bytes 8388608
  1092.3 113.6 %copy-start.6 = (bf16[256,2048]{1,0:T(8,128)(2,1)S(1)}, bf16[256,2048]{1,0:T(8,128)(2,1)}, u32[]{:S(2)}) copy-start(bf16[256,2048]{1,0:T(8,128)(2,1)} %param.24) | copy-start | bytes 3145732
  1092.3 113.6 %copy-start.29 = (f32[2048]{0:T(1024)S(1)}, f32[2048]{0:T(1024)}, u32[]{:S(2)}) copy-start(f32[2048]{0:T(1024)} %param.25) | copy-start | bytes 24580
  1092.3 113.6 %copy-start.32 = (f32[256]{0:T(256)S(1)}, f32[256]{0:T(256)}, u32[]{:S(2)}) copy-start(f32[256]{0:T(256)} %copy-done.31) | copy-start | bytes 3076
  1093.5 114.6 %copy-start.41 = (f32[256]{0:T(256)S(1)}, f32[256]{0:T(256)}, u32[]{:S(2)}) copy-start(f32[256]{0:T(256)} %copy-done.40) | copy-start | bytes 3076
  1093.5 114.7 %copy-start.37 = (f32[256]{0:T(256)S(1)}, f32[256]{0:T(256)}, u32[]{:S(2)}) copy-start(f32[256]{0:T(256)} %copy-done.36) | copy-start | bytes 3076
  1093.5 115.6 %copy-start.12 = (bf16[256,2048]{1,0:T(8,128)(2,1)S(1)}, bf16[256,2048]{1,0:T(8,128)(2,1)}, u32[]{:S(2)}) copy-start(bf16[256,2048]{1,0:T(8,128)(2,1)} %param.40) | copy-start | bytes 3145732
  1093.5 115.6 %copy-start.39 = (f32[256]{0:T(256)S(1)}, f32[256]{0:T(256)}, u32[]{:S(2)}) copy-start(f32[256]{0:T(256)} %copy-done.38) | copy-start | bytes 3076
  1093.5 115.6 %copy-start.43 = (f32[256]{0:T(256)S(1)}, f32[256]{0:T(256)}, u32[]{:S(2)}) copy-start(f32[256]{0:T(256)} %copy-done.42) | copy-start | bytes 3076
  (59 other events, 226.4 us)
Sparse Core Ops, SparseCore 0:
  14.4 84.7 all-gather.4
  187.2 166.6 reduce-scatter.4
  358.8 80.4 all-gather.6
  441.3 80.5 all-gather.8
  557.2 166.6 reduce-scatter.8
  726.6 87.9 reduce-scatter.6
  822.1 80.4 all-gather.10
  1039.2 166.6 reduce-scatter.10
  1211.6 442.9 all-reduce.4
where the time goes:
time: 1690 us; the launch traced here: 1680 us
  waiting for transfers between devices  1210 us (72%)
  matrix products  259 us (15%)
  other arithmetic  64.5 us (4%)
  local copies, waits for them, and re-layouts  58.9 us (3%)
  blocking collectives  51.1 us (3%)
    psum x1, waiting for transfers between devices, on_device(): lax.psum((grad_query, grad_query_bias, grad_key, grad_value, grad_value_b...  401 us
    reduce_scatter x1, waiting for transfers between devices, on_device(): lax.psum_scatter(jnp.dot(attended, w_out, preferred_element_type=jnp.floa...  167 us
    reduce_scatter x1, waiting for transfers between devices, on_device(): lax.psum_scatter(times_transpose(hidden_cot, w_up), 'mp', scatter_dimensi...  151 us
    reduce_scatter x1, waiting for transfers between devices, on_device(): lax.psum_scatter(times_transpose(query_low, w_query) + times_transpose(ke...  101 us
    reduce_scatter x1, waiting for transfers between devices, on_device(): lax.psum_scatter(jnp.dot(activated, w_down, preferred_element_type=jnp.fl...  87.2 us
    all_gather x1, waiting for transfers between devices, on_device(): gathered_one = lax.all_gather(normed_one, 'mp', axis=0, tiled=True)  84.8 us
    all_gather x1, waiting for transfers between devices, on_device(): gathered_branch = lax.all_gather(branch_cot, 'mp', axis=0, tiled=True)  78.8 us
    all_gather x1, waiting for transfers between devices, on_device(): gathered_two = lax.all_gather(normed_two, 'mp', axis=0, tiled=True)  76 us
  transfers between devices with their start and end apart: 9, of which 9 were waited for; matrix products, arithmetic and copies ran while one was open for 6% of the time, Pallas kernels for 0%

commit v1 on v0

--- a/solution.py
+++ b/solution.py
@@ -6,6 +6,27 @@
 HD = 128
 BLOCK = 256
 epsilon = 1e-05
+
+
+def joined_along(blocks, dim):
+    blocks = jnp.moveaxis(blocks, 0, dim)
+    dims = blocks.shape
+    return blocks.reshape(*dims[:dim], dims[dim] * dims[dim + 1], *dims[dim + 2 :])
+
+
+def doubled(x, axis):
+    length, index = (lax.axis_size(axis), lax.axis_index(axis))
+    blocks, stride = (x[None], 1)
+    while stride < length:
+        theirs = lax.ppermute(blocks, axis, [(i, i ^ stride) for i in range(length)])
+        low = index & stride == 0
+        blocks = jnp.concatenate([jnp.where(low, blocks, theirs), jnp.where(low, theirs, blocks)])
+        stride *= 2
+    return blocks
+
+
+def doubled_up(array, axis, dim):
+    return joined_along(doubled(array, axis), dim)
 
 
 def layer_norm(values, gain, bias):
@@ -168,7 +189,7 @@
     middle_cot = out_cot + middle_part
     grad_out_bias = jnp.sum(middle_cot, axis=0)
     branch_cot = middle_cot.astype(jnp.bfloat16)
-    gathered_branch = lax.all_gather(branch_cot, "mp", axis=0, tiled=True)
+    gathered_branch = doubled_up(branch_cot, "mp", 0)
     attended_cot = times_transpose(gathered_branch, w_out).astype(jnp.bfloat16)
     grad_out = inner_rows(attended, gathered_branch)
     attended_cot = attended_cot.reshape(head_shape)

time: 1690 us -> 1860 us (1.10)
  waiting for transfers between devices: 1210 us -> 1370 us
  other arithmetic: 64.5 us -> 85.6 us
    ppermute x0 -> x3, waiting for transfers between devices: none -> 231 us  [doubled(): lax.ppermute(blocks, axis, [(i, i ^ stride) for i in range(length)])]
    all_gather x1 -> x0, waiting for transfers between devices: 78.8 us -> none  [on_device(): gathered_branch = lax.all_gather(branch_cot, 'mp', axis=0, tiled=True)]
  transfers between devices with their start and end apart: 9 -> 11, of which waited for: 9 -> 11; matrix products, arithmetic and copies ran while one was open for 6% -> 5% of each run, Pallas kernels for 0% -> 0%
where the time goes in v1:
time: 1860 us
  waiting for transfers between devices  1370 us (74%)
  matrix products  259 us (14%)
  other arithmetic  85.6 us (5%)
  local copies, waits for them, and re-layouts  60.6 us (3%)
  blocking collectives  51.1 us (3%)
    psum x1, waiting for transfers between devices, on_device(): lax.psum((grad_query, grad_query_bias, grad_key, grad_value, grad_value_b...  401 us
    ppermute x3, waiting for transfers between devices, doubled(): lax.ppermute(blocks, axis, [(i, i ^ stride) for i in range(length)])  231 us
    reduce_scatter x1, waiting for transfers between devices, on_device(): lax.psum_scatter(jnp.dot(attended, w_out, preferred_element_type=jnp.floa...  167 us
    reduce_scatter x1, waiting for transfers between devices, on_device(): lax.psum_scatter(times_transpose(hidden_cot, w_up), 'mp', scatter_dimensi...  151 us
    reduce_scatter x1, waiting for transfers between devices, on_device(): lax.psum_scatter(times_transpose(query_low, w_query) + times_transpose(ke...  101 us
    reduce_scatter x1, waiting for transfers between devices, on_device(): lax.psum_scatter(jnp.dot(activated, w_down, preferred_element_type=jnp.fl...  87.2 us
    all_gather x1, waiting for transfers between devices, on_device(): gathered_one = lax.all_gather(normed_one, 'mp', axis=0, tiled=True)  84.8 us
    all_gather x1, waiting for transfers between devices, on_device(): gathered_two = lax.all_gather(normed_two, 'mp', axis=0, tiled=True)  76 us
  transfers between devices with their start and end apart: 11, of which 11 were waited for; matrix products, arithmetic and copies ran while one was open for 5% of the time, Pallas kernels for 0%

profile of v1, /device:TPU:0, one launch (start us, length us, event | category | flops | bytes accessed | tf_op | source)
XLA Modules:
  0.0 1855.7 jit_solution(12782029724336403883)
XLA Ops:
  14.5 84.8 %all-gather.4.cloned.1.call-done = bf16[2048,2048]{1,0:T(8,128)(2,1)} async-done(((bf16[256,2048]{1,0:T(8,128)(2,1)}), bf16[2048,2048]{1,0:T(8,128)(2,1)}) %all-gather.4.cloned.1.call-update) | async-done | bytes 8388624 | tf_op jit(solution)/shard_map/all_gather | solution.py:104
  99.3 6.7 convolution_convert_fusion.2
  107.7 6.7 fusion.51
  116.0 7.0 fusion.52
  123.1 54.4 %while.31 = (s32[]{:T(128)}, bf16[4,512,256]{2,1,0:T(8,128)(2,1)}, f32[4,2,512]{2,1,0:T(2,128)S(1)}, s32[4]{0:T(128)S(1)}, s32[2048]{0:T(1024)S(1)}, /*index=5*/...) while((s32[]{:T(128)}, bf16[4,512,256]{2,1,0:T(8,128)(2,1)}, ...), condition=%wide.region_5.6_spmd, body=%wide.region_2.5_spmd.sunk | while | flops 1103232512 | bytes 41470496 | solution.py:142
  177.5 9.8 fusion.81
  187.4 166.7 %reduce-scatter.5.cloned.1.call-done = f32[256,2048]{1,0:T(8,128)} async-done(((f32[2048,2048]{1,0:T(8,128)}), f32[256,2048]{1,0:T(8,128)}) %reduce-scatter.5.cloned.1.call-update) | async-done | bytes 2097168 | tf_op jit(solution)/shard_map/reduce_scatter | solution.py:144
  363.6 76.0 %all-gather.6.cloned.1.call-done = bf16[2048,2048]{1,0:T(8,128)(2,1)} async-done(((bf16[256,2048]{1,0:T(8,128)(2,1)}), bf16[2048,2048]{1,0:T(8,128)(2,1)}) %all-gather.6.cloned.1.call-update) | async-done | bytes 8388624 | tf_op jit(solution)/shard_map/all_gather | solution.py:153
  439.5 14.7 fusion.82
  454.2 67.9 %all-gather.8.cloned.1.call-done = bf16[2048,2048]{1,0:T(8,128)(2,1)} async-done(((bf16[256,2048]{1,0:T(8,128)(2,1)}), bf16[2048,2048]{1,0:T(8,128)(2,1)}) %all-gather.8.cloned.1.call-update) | async-done | bytes 8388624 | tf_op jit(solution)/shard_map/all_gather | solution.py:179
  522.1 20.8 %convert_reduce_fusion = (f32[1024]{0:T(1024)}, bf16[2048,1024]{1,0:T(8,128)(2,1)S(1)}) fusion(f32[2048,1024]{1,0:T(8,128)} %fusion.82, f32[1024]{0:T(1024)S(1)} %copy-done.53, bf16[2048,2048]{1,0:T(8,128)(2,1)} %all-gather.8.cloned.1.call-done, bf16[1024,2048]{1,0:T(8,128)(2,1)} %param.38), kind=kOutput, calls=%fused_computation.63 | convolution fusion | flops 8638168064 | bytes 25174016 | tf_op jit(solution)/shard_map/dot_general | solution.py:46
  545.0 12.1 fusion.83
  557.2 15.5 convolution_convert_fusion
  572.7 151.2 %reduce-scatter.9.cloned.1.call-done = f32[256,2048]{1,0:T(8,128)} async-done(((f32[2048,2048]{1,0:T(8,128)}), f32[256,2048]{1,0:T(8,128)}) %reduce-scatter.9.cloned.1.call-update) | async-done | bytes 2097168 | tf_op jit(solution)/shard_map/reduce_scatter | solution.py:185
  727.5 87.2 %reduce-scatter.7.cloned.1.call-done = bf16[256,2048]{1,0:T(8,128)(2,1)} async-done(((bf16[2048,2048]{1,0:T(8,128)(2,1)}), bf16[256,2048]{1,0:T(8,128)(2,1)}) %reduce-scatter.7.cloned.1.call-update) | async-done | bytes 1048592 | tf_op jit(solution)/shard_map/reduce_scatter | solution.py:159
  829.2 48.0 %collective-permute-done.1 = bf16[2,256,2048]{2,1,0:T(8,128)(2,1)} collective-permute-done((bf16[2,256,2048]{2,1,0:T(8,128)(2,1)}, bf16[2,256,2048]{2,1,0:T(8,128)(2,1)}, u32[]{:S(2)}, u32[]{:S(2)}) %collective-permute-start.1) | collective-permute-done | bytes 2097184 | tf_op jit(solution)/shard_map/ppermute | solution.py:21
  884.9 180.5 %collective-permute-done.2 = bf16[4,256,2048]{2,1,0:T(8,128)(2,1)} collective-permute-done((bf16[4,256,2048]{2,1,0:T(8,128)(2,1)}, bf16[4,256,2048]{2,1,0:T(8,128)(2,1)}, u32[]{:S(2)}, u32[]{:S(2)}) %collective-permute-start.2) | collective-permute-done | bytes 4194336 | tf_op jit(solution)/shard_map/ppermute | solution.py:21
  1065.4 5.7 broadcast_select_fusion.1
  1071.1 7.6 pad_maximum_fusion
  1078.7 6.7 convolution_convert_fusion.1
  1085.4 88.9 %while.32 = (s32[]{:T(128)}, f32[2048,2,128]{0,2,1:T(8,128)}, f32[2048,2,128]{0,2,1:T(8,128)}, bf16[4,512,2,128]{3,1,2,0:T(8,128)(2,1)}, s32[4]{0:T(128)S(1)}, /...) while((s32[]{:T(128)}, f32[2048,2,128]{0,2,1:T(8,128)}, ...), condition=%wide.region_18.19_spmd.clone, body=%wide.region_16.18_spmd.clone.sunk | while | flops 2722758144 | bytes 118012680 | solution.py:232
  1136.1 4.8 fusion.168
  1180.3 8.2 fusion.84
  1188.5 8.2 fusion.65
  1196.7 18.5 add_add_fusion
  1215.3 15.2 fusion.88
  1230.5 19.1 %fusion.75 = f32[1024,2048]{1,0:T(8,128)} fusion(bf16[2048,2048]{1,0:T(8,128)(2,1)} %all-gather.8.cloned.1.call-done, f32[2048,1024]{1,0:T(8,128)} %fusion.82, f32[1024]{0:T(1024)S(1)} %copy-done.54), kind=kOutput, calls=%fused_computation.134 | convolution fusion | flops 8610906112 | bytes 25169920 | tf_op jit(solution)/shard_map/dot_general | solution.py:40
  1249.7 7.2 fusion.87
  1269.9 10.9 all-reduce.1
  1280.8 101.2 %reduce-scatter.11.cloned.1.call-done = f32[256,2048]{1,0:T(8,128)} async-done(((f32[2048,2048]{1,0:T(8,128)}), f32[256,2048]{1,0:T(8,128)}) %reduce-scatter.11.cloned.1.call-update) | async-done | bytes 2097168 | tf_op jit(solution)/shard_map/reduce_scatter | solution.py:243
  1389.6 40.2 %all-reduce = (f32[2048]{0:T(1024)}, f32[2048]{0:T(1024)}, f32[2048]{0:T(1024)}, f32[2048]{0:T(1024)}, f32[2048]{0:T(1024)}, /*index=5*/f32[2048]{0:T(1024)}) all-reduce(f32[2048]{0:T(1024)S(1)} %get-tuple-element.403, f32[2048]{0:T(1024)S(1)} %get-tuple-element.406, ...), channel_id=1, replica_groups=mesh['dp'=4,'mp'=8] {'dp','mp'}, use_global_device_ids=true, to_apply=%region_23.24 | all-reduce | flops 12288 | bytes 98304 | tf_op jit(solution)/shard_map/psum | solution.py:253
  1429.8 400.9 %all-reduce.5.cloned.1.call-done = (f32[2048,256]{1,0:T(8,128)}, f32[2048,256]{1,0:T(8,128)}, f32[2048,256]{1,0:T(8,128)}, f32[256,2048]{1,0:T(8,128)}, f32[2048,1024]{1,0:T(8,128)}, /*index=5*/f32[1024,2048]{1,0:T(8,128)}) async-done(((f32[2048,256]{1,0:T(8,128)}, f32[2048,256]{1,0:T(8,128)}, f32[2048,256]{1,0:T(8,128)}, f32[256,2048]{1,0:T(8,128)}, f32[2048,1024]{1,0:T(8,128)}, ...) | async-done | bytes 25165840 | tf_op jit(solution)/shard_map/psum | solution.py:257
  (351 shorter events, 215.1 us)
Async XLA Ops:
  7.2 170.3 %copy-start = (bf16[256,2048]{1,0:T(8,128)(2,1)S(1)}, bf16[256,2048]{1,0:T(8,128)(2,1)}, u32[]{:S(2)}) copy-start(bf16[256,2048]{1,0:T(8,128)(2,1)} %param.32) | copy-start | bytes 3145732
  7.2 92.1 %copy-start.27 = (bf16[2048,256]{1,0:T(8,128)(2,1)S(1)}, bf16[2048,256]{1,0:T(8,128)(2,1)}, u32[]{:S(2)}) copy-start(bf16[2048,256]{1,0:T(8,128)(2,1)} %param.29) | copy-start | bytes 3145732
  7.2 92.1 %all-gather.4.cloned.1.call-start = ((), (), s32[]{:S(2)}) async-start(), calls=%async_computation.4 | async-start | bytes 9437184 | tf_op jit(solution)/shard_map/all_gather | solution.py:104
  14.4 339.8 %reduce-scatter.5.cloned.1.call-start = ((), (), s32[]{:S(2)}) async-start(), calls=%async_computation.5 | async-start | bytes 18874368 | tf_op jit(solution)/shard_map/reduce_scatter | solution.py:144
  14.4 93.2 %copy-start.29 = (bf16[2048,256]{1,0:T(8,128)(2,1)S(1)}, bf16[2048,256]{1,0:T(8,128)(2,1)}, u32[]{:S(2)}) copy-start(bf16[2048,256]{1,0:T(8,128)(2,1)} %param.27) | copy-start | bytes 3145732
  14.4 93.2 %copy-start.55 = (f32[256]{0:T(256)S(1)}, f32[256]{0:T(256)}, u32[]{:S(2)}) copy-start(f32[256]{0:T(256)} %param.28) | copy-start | bytes 3076
  187.3 166.8 %copy-start.5 = (bf16[256,2048]{1,0:T(8,128)(2,1)S(1)}, bf16[256,2048]{1,0:T(8,128)(2,1)}, u32[]{:S(2)}) copy-start(bf16[256,2048]{1,0:T(8,128)(2,1)} %param.24) | copy-start | bytes 3145732
  187.3 166.8 %copy-start.47 = (f32[2048]{0:T(1024)S(1)}, f32[2048]{0:T(1024)}, u32[]{:S(2)}) copy-start(f32[2048]{0:T(1024)} %param.33) | copy-start | bytes 24580
  187.3 170.1 %copy-start.33 = (f32[2048]{0:T(1024)S(1)}, f32[2048]{0:T(1024)}, u32[]{:S(2)}) copy-start(f32[2048]{0:T(1024)} %param.34) | copy-start | bytes 24580
  187.3 170.1 %copy-start.48 = (f32[2048]{0:T(1024)S(1)}, f32[2048]{0:T(1024)}, u32[]{:S(2)}) copy-start(f32[2048]{0:T(1024)} %param.35) | copy-start | bytes 24580
  187.4 252.2 %all-gather.6.cloned.1.call-start = ((), (), s32[]{:S(2)}) async-start(), calls=%async_computation.6 | async-start | bytes 9437184 | tf_op jit(solution)/shard_map/all_gather | solution.py:153
  358.9 163.2 %all-gather.8.cloned.1.call-start = ((), (), s32[]{:S(2)}) async-start(), calls=%async_computation.8 | async-start | bytes 9437184 | tf_op jit(solution)/shard_map/all_gather | solution.py:179
  362.2 457.0 %copy-start.41 = (f32[256]{0:T(256)}, f32[256]{0:T(256)S(1)}, u32[]{:S(2)}) copy-start(f32[256]{0:T(256)S(1)} %compare_convert_fusion) | copy-start | bytes 3076
  363.5 158.6 %copy-start.53 = (f32[1024]{0:T(1024)S(1)}, f32[1024]{0:T(1024)}, u32[]{:S(2)}) copy-start(f32[1024]{0:T(1024)} %param.37) | copy-start | bytes 12292
  363.5 360.4 %reduce-scatter.9.cloned.1.call-start = ((), (), s32[]{:S(2)}) async-start(), calls=%async_computation.9 | async-start | bytes 18874368 | tf_op jit(solution)/shard_map/reduce_scatter | solution.py:185
  557.1 257.5 %reduce-scatter.7.cloned.1.call-start = ((), (), s32[]{:S(2)}) async-start(), calls=%async_computation.7 | async-start | bytes 9437184 | tf_op jit(solution)/shard_map/reduce_scatter | solution.py:159
  572.7 242.0 %copy-start.49 = (f32[2048]{0:T(1024)S(1)}, f32[2048]{0:T(1024)}, u32[]{:S(2)}) copy-start(f32[2048]{0:T(1024)} %param.39) | copy-start | bytes 24580
  572.7 809.4 %reduce-scatter.11.cloned.1.call-start = ((), (), s32[]{:S(2)}) async-start(), calls=%async_computation.10 | async-start | bytes 18874368 | tf_op jit(solution)/shard_map/reduce_scatter | solution.py:243
  822.0 3.0 collective-permute-start
  829.2 48.0 %collective-permute-start.1 = (bf16[2,256,2048]{2,1,0:T(8,128)(2,1)}, bf16[2,256,2048]{2,1,0:T(8,128)(2,1)}, u32[]{:S(2)}, u32[]{:S(2)}) collective-permute-start(bf16[2,256,2048]{2,1,0:T(8,128)(2,1)} %pad_maximum_fusion.2), channel_id=1, source_target_pairs={{0,2},{1,3},{2,0},{3,1},{4,6},{5,7},{6,4},{7,5},{8,10},{9,11},{10,... | collective-permute-start | bytes 6291464 | tf_op jit(solution)/shard_map/ppermute | solution.py:21
  882.6 182.9 %collective-permute-start.2 = (bf16[4,256,2048]{2,1,0:T(8,128)(2,1)}, bf16[4,256,2048]{2,1,0:T(8,128)(2,1)}, u32[]{:S(2)}, u32[]{:S(2)}) collective-permute-start(bf16[4,256,2048]{2,1,0:T(8,128)(2,1)} %pad_maximum_fusion.1), channel_id=1, source_target_pairs={{0,4},{1,5},{2,6},{3,7},{4,0},{5,1},{6,2},{7,3},{8,12},{9,13},{10,... | collective-permute-start | bytes 12582920 | tf_op jit(solution)/shard_map/ppermute | solution.py:21
  1215.3 615.4 %all-reduce.5.cloned.1.call-start = ((), (), s32[]{:S(2)}) async-start(), calls=%async_computation.11 | async-start | bytes 50331648 | tf_op jit(solution)/shard_map/psum | solution.py:257
  1215.3 41.6 %slice-start.4 = ((s8[8388608]{0:T(1024)(128)(4,1)}), s8[4194304]{0:T(1024)(128)(4,1)S(1)}, s32[]{:S(2)}) async-start(s8[8388608]{0:T(1024)(128)(4,1)} %bitcast.167), calls=%async_computation.16 | async-start | bytes 8388608
  1230.5 26.3 %slice-start.5 = ((s8[8388608]{0:T(1024)(128)(4,1)}), s8[4194304]{0:T(1024)(128)(4,1)S(1)}, s32[]{:S(2)}) async-start(s8[8388608]{0:T(1024)(128)(4,1)} %bitcast.167), calls=%async_computation.17 | async-start | bytes 8388608
  1268.4 113.6 %copy-start.6 = (bf16[256,2048]{1,0:T(8,128)(2,1)S(1)}, bf16[256,2048]{1,0:T(8,128)(2,1)}, u32[]{:S(2)}) copy-start(bf16[256,2048]{1,0:T(8,128)(2,1)} %param.24) | copy-start | bytes 3145732
  1268.4 113.6 %copy-start.32 = (f32[2048]{0:T(1024)S(1)}, f32[2048]{0:T(1024)}, u32[]{:S(2)}) copy-start(f32[2048]{0:T(1024)} %param.25) | copy-start | bytes 24580
  1268.4 113.6 %copy-start.35 = (f32[256]{0:T(256)S(1)}, f32[256]{0:T(256)}, u32[]{:S(2)}) copy-start(f32[256]{0:T(256)} %copy-done.34) | copy-start | bytes 3076
  1269.6 114.7 %copy-start.44 = (f32[256]{0:T(256)S(1)}, f32[256]{0:T(256)}, u32[]{:S(2)}) copy-start(f32[256]{0:T(256)} %copy-done.43) | copy-start | bytes 3076
  1269.6 114.7 %copy-start.40 = (f32[256]{0:T(256)S(1)}, f32[256]{0:T(256)}, u32[]{:S(2)}) copy-start(f32[256]{0:T(256)} %copy-done.39) | copy-start | bytes 3076
  1269.6 115.7 %copy-start.15 = (bf16[256,2048]{1,0:T(8,128)(2,1)S(1)}, bf16[256,2048]{1,0:T(8,128)(2,1)}, u32[]{:S(2)}) copy-start(bf16[256,2048]{1,0:T(8,128)(2,1)} %param.40) | copy-start | bytes 3145732
  1269.6 115.7 %copy-start.42 = (f32[256]{0:T(256)S(1)}, f32[256]{0:T(256)}, u32[]{:S(2)}) copy-start(f32[256]{0:T(256)} %copy-done.41) | copy-start | bytes 3076
  1269.6 115.7 %copy-start.46 = (f32[256]{0:T(256)S(1)}, f32[256]{0:T(256)}, u32[]{:S(2)}) copy-start(f32[256]{0:T(256)} %copy-done.45) | copy-start | bytes 3076
  (64 other events, 263.8 us)
Sparse Core Ops, SparseCore 0:
  14.5 84.7 all-gather.3
  187.5 166.6 reduce-scatter.4
  359.0 80.4 all-gather.5
  441.6 80.5 all-gather.7
  557.3 166.6 reduce-scatter.8
  726.7 87.9 reduce-scatter.6
  1215.4 166.6 reduce-scatter.10
  1387.7 442.9 all-reduce.4
